TPU v7x, 128 devices: a whole 4x4x4 slice. The times are simulated.
128 devices in a mesh: section: 2 (over core), blk: 16 (over y, x), mp: 4 (over z).
Axes of the slice: x: 4, y: 4, z: 4, core: 2. Of those that a mesh axis runs over, the one named last changes fastest.
Arguments:
- patches: bfloat16 [256, 5120], P('section'), may hold values from -6 to 6
- merge_gain: float32 [1280], replicated, may hold values from 0.25 to 1.75
- merge_first: bfloat16 [5120, 5120], P(None, ('blk', 'mp')), may hold values from -0.078125 to 0.078125
- merge_second: bfloat16 [5120, 4096], P(('blk', 'mp')), may hold values from -0.078125 to 0.078125
- text_embeds: bfloat16 [4, 1024, 4096], P(None, 'blk', 'mp'), may hold values from -7 to 14
- positions: int32 [256], replicated, may hold values from 0 to 4095, as said below
- segments: int32 [4096], replicated, may hold values from 0 to 2, never falling along the last dimension, each value on 1 to 2048 neighbouring positions
- norm_gain: float32 [2, 4096], P('section'), may hold values from 0.25 to 1.75
- query_weight: bfloat16 [2, 4096, 4096], P('section', 'blk', 'mp'), may hold values from -1 to 1
- keyval_weight: bfloat16 [2, 4096, 4, 2, 128], P('section', 'blk', 'mp'), may hold values from -1 to 1
- out_weight: bfloat16 [2, 4096, 4096], P('section', 'mp', 'blk'), may hold values from -0.09375 to 0.09375
Outputs:
- hidden: bfloat16 [2, 4, 1024, 4096], P('section', None, 'blk', 'mp')
Inputs may be any that keep to these rules, and one draw needn't show every extreme that they name: `positions`: distinct and increasing.
All inputs are finite; a program needn't handle non-finite values.
Results may differ from a plain program's by a relative error of at most 0.015.
Values may be sent and summed in bfloat16 or wider, within the bound.
No kernel may reach another device: no remote copies, remote signals or barrier semaphores. Data moves between devices by JAX's collectives and lax.ppermute only.
A program may use at most 128 MiB of HBM per device.

v0:
```python
import jax
import jax.numpy as jnp
from jax import lax
from jax.sharding import PartitionSpec as P

epsilon = 1e-06
rope_base = 1000000.0


def shifted(value, axis, by):
    size = lax.axis_size(axis)
    pairs = [(i, i + by) for i in range(size) if 0 <= i + by < size]
    return lax.ppermute(value, axis, pairs)


def rope_tables(where_at, head_size):
    steps_half = jnp.arange(head_size // 2).astype(jnp.float32)
    inverse = jnp.exp(-jnp.log(rope_base) * 2.0 * steps_half / head_size)
    angles = where_at.astype(jnp.float32)[:, None] * inverse[None, :]
    return (jnp.cos(angles), jnp.sin(angles))


def rotate(values, cosine, sine):
    half = values.shape[-1] // 2
    first = values[..., :half]
    second = values[..., half:]
    cosine = cosine[:, None, :]
    sine = sine[:, None, :]
    return jnp.concatenate(
        [first * cosine - second * sine, second * cosine + first * sine], axis=-1
    )


def local(
    patches,
    merge_gain,
    merge_first,
    merge_second,
    text_embeds,
    positions,
    segments,
    norm_gain,
    query_weight,
    keyval_weight,
    out_weight,
):
    count = patches.shape[0]
    width = merge_gain.shape[0]
    blocks = text_embeds.shape[0]
    rows_here = text_embeds.shape[1]
    slice_width = text_embeds.shape[2]
    seq_len = segments.shape[0]
    block_len = seq_len // blocks
    section_index = lax.axis_index("section")
    cycle_index = lax.axis_index("blk")
    model_index = lax.axis_index("mp")
    pieces = patches.astype(jnp.float32).reshape(count, -1, width)
    centered = pieces - jnp.mean(pieces, axis=-1, keepdims=True)
    variance = jnp.mean(centered * centered, axis=-1, keepdims=True)
    normed = (
        (centered * lax.rsqrt(variance + epsilon) * merge_gain)
        .reshape(count, -1)
        .astype(jnp.bfloat16)
    )
    inner = jax.nn.gelu(
        jnp.dot(normed, merge_first, preferred_element_type=jnp.float32), approximate=False
    ).astype(jnp.bfloat16)
    partial_merge = jnp.dot(inner, merge_second, preferred_element_type=jnp.float32)
    merged_full = lax.psum(partial_merge, ("blk", "mp")).astype(jnp.bfloat16)
    merged_mine = lax.dynamic_slice_in_dim(merged_full, model_index * slice_width, slice_width, 1)
    visual_all = lax.all_gather(merged_mine, "section", axis=0, tiled=True)
    query_full, keyval_full, out_full = (
        lax.all_gather(query_weight, "blk", axis=1, tiled=True),
        lax.all_gather(keyval_weight, "blk", axis=1, tiled=True),
        lax.all_gather(out_weight, "blk", axis=2, tiled=True),
    )
    query_full = query_full[0]
    kv_heads = keyval_full.shape[2]
    head_size = keyval_full.shape[4]
    keyval_full = keyval_full[0].reshape(keyval_full.shape[1], -1)
    out_full = out_full[0]
    gain_here = norm_gain[0]
    group = query_full.shape[1] // (kv_heads * head_size)
    scale = 1.0 / head_size**0.5
    key_where = jnp.arange(seq_len)
    ticks = blocks + lax.axis_size("section") - 1
    zero_index = jnp.zeros((), jnp.int32)
    held = jnp.zeros((rows_here, slice_width), jnp.bfloat16)
    cache_keys = jnp.zeros((seq_len, kv_heads, head_size), jnp.bfloat16)
    cache_values = jnp.zeros((seq_len, kv_heads, head_size), jnp.bfloat16)
    outputs = jnp.zeros((blocks, rows_here, slice_width), jnp.bfloat16)
    for tick_now in range(ticks):
        bound = min(tick_now + 1, blocks) * block_len
        block_now = tick_now - section_index
        active = (block_now >= 0) & (block_now < blocks)
        block_safe = jnp.clip(block_now, 0, blocks - 1)
        row_where = block_safe * block_len + cycle_index * rows_here + jnp.arange(rows_here)
        is_visual = positions[None, :] == row_where[:, None]
        picked = jnp.dot(
            is_visual.astype(jnp.bfloat16), visual_all, preferred_element_type=jnp.float32
        ).astype(jnp.bfloat16)
        text_rows = lax.dynamic_index_in_dim(text_embeds, block_safe, 0, keepdims=False)
        embedded = jnp.where(jnp.any(is_visual, axis=1)[:, None], picked, text_rows)
        incoming = jnp.where(section_index == 0, embedded, held)
        features = lax.all_gather(incoming, "mp", axis=1, tiled=True)
        feat_f = features.astype(jnp.float32)
        normx = (
            feat_f
            * lax.rsqrt(jnp.mean(feat_f * feat_f, axis=-1, keepdims=True) + epsilon)
            * gain_here
        ).astype(jnp.bfloat16)
        cosine, sine = rope_tables(row_where, head_size)
        query = jnp.dot(normx, query_full, preferred_element_type=jnp.float32).reshape(
            rows_here, -1, head_size
        )
        query = (
            rotate(query, cosine, sine)
            .astype(jnp.bfloat16)
            .reshape(rows_here, kv_heads, group, head_size)
        )
        keyval = jnp.dot(normx, keyval_full, preferred_element_type=jnp.float32).reshape(
            rows_here, kv_heads, 2, head_size
        )
        new_keys = rotate(keyval[:, :, 0, :], cosine, sine).astype(jnp.bfloat16)
        new_values = keyval[:, :, 1, :].astype(jnp.bfloat16)
        block_keys, block_values = (
            lax.all_gather(new_keys, "blk", axis=0, tiled=True),
            lax.all_gather(new_values, "blk", axis=0, tiled=True),
        )
        start = block_safe * block_len
        cache_keys = jnp.where(
            active,
            lax.dynamic_update_slice(cache_keys, block_keys, (start, zero_index, zero_index)),
            cache_keys,
        )
        cache_values = jnp.where(
            active,
            lax.dynamic_update_slice(cache_values, block_values, (start, zero_index, zero_index)),
            cache_values,
        )
        keys_seen = cache_keys[:bound]
        values_seen = cache_values[:bound]
        scores = (
            jnp.einsum("qkgd,skd->kgqs", query, keys_seen, preferred_element_type=jnp.float32)
            * scale
        )
        row_segments = jnp.take(segments, row_where)
        allowed = (key_where[None, :bound] <= row_where[:, None]) & (
            segments[None, :bound] == row_segments[:, None]
        )
        scores = jnp.where(allowed[None, None], scores, -jnp.inf)
        top = jnp.max(scores, axis=-1, keepdims=True)
        expo = jnp.exp(scores - top)
        probs = (expo / jnp.sum(expo, axis=-1, keepdims=True)).astype(jnp.bfloat16)
        attended = jnp.einsum(
            "kgqs,skd->qkgd", probs, values_seen, preferred_element_type=jnp.float32
        )
        attended = attended.reshape(rows_here, -1).astype(jnp.bfloat16)
        term = jnp.dot(attended, out_full, preferred_element_type=jnp.float32)
        summed = lax.psum_scatter(
            term.astype(jnp.bfloat16), "mp", scatter_dimension=1, tiled=True
        ).astype(jnp.float32)
        result = (incoming.astype(jnp.float32) + summed).astype(jnp.bfloat16)
        outputs = jnp.where(
            active,
            lax.dynamic_update_slice(outputs, result[None], (block_safe, zero_index, zero_index)),
            outputs,
        )
        held = shifted(result, "section", 1)
    return outputs[None]


def solution(mesh):
    return jax.shard_map(
        local,
        mesh=mesh,
        in_specs=(
            P("section", None),
            P(),
            P(None, ("blk", "mp")),
            P(("blk", "mp"), None),
            P(None, "blk", "mp"),
            P(),
            P(),
            P("section", None),
            P("section", "blk", "mp"),
            P("section", "blk", "mp", None, None),
            P("section", "mp", "blk"),
        ),
        out_specs=P("section", None, "blk", "mp"),
        check_vma=False,
    )
```

profile of v0, /device:TPU:0, one launch (start us, length us, event | category | flops | bytes accessed | tf_op | source)
XLA Modules:
  0.0 948.9 jit_solution(6913599249277682439)
XLA Ops:
  8.8 2.9 reshape.1266
  16.2 5.2 fusion.210
  23.5 383.3 %all-reduce.1 = bf16[128,4096]{1,0:T(8,128)(2,1)S(1)} all-reduce(f32[128,4096]{1,0:T(8,128)} %fusion.210), channel_id=1, replica_groups=mesh['section'=2,'blk'=16,'mp'=4] {'blk','mp'}, use_global_device_ids=true, to_apply=%region_3.4 | all-reduce | flops 524288 | bytes 3145728 | tf_op jit(solution)/shard_map/psum | solution.py:69
  411.0 13.4 %all_gather.58 = bf16[64,4096]{1,0:T(8,128)(2,1)S(1)} all-gather(bf16[64,1024]{1,0:T(8,128)(2,1)S(1)} %fusion.63), channel_id=1, replica_groups=mesh['section'=2,'blk'=16,'mp'=4] {'mp'}, dimensions={1}, use_global_device_ids=true | all-gather | bytes 655360 | tf_op jit(solution)/shard_map/all_gather | solution.py:105
  426.1 4.7 copy.37
  432.0 20.7 %all_gather.61 = bf16[1024,1,128]{2,0,1:T(8,128)(2,1)S(1)} all-gather(bf16[64,1,128]{2,0,1:T(8,128)(2,1)S(1)} %pad_maximum_fusion), channel_id=1, replica_groups=mesh['section'=2,'blk'=16,'mp'=4] {'blk'}, dimensions={0}, use_global_device_ids=true | all-gather | bytes 278528 | tf_op jit(solution)/shard_map/all_gather | solution.py:127
  452.7 24.1 %all-gather = bf16[1024,1,1,128]{3,0,2,1:T(8,128)(2,1)S(1)} all-gather(bf16[64,1,1,128]{3,0,2,1:T(8,128)(2,1)S(1)} %slice.285), channel_id=2, replica_groups=mesh['section'=2,'blk'=16,'mp'=4] {'blk'}, dimensions={0}, use_global_device_ids=true | all-gather | bytes 278528 | tf_op jit(solution)/shard_map/all_gather | solution.py:128
  480.5 11.8 %copy.31 = bf16[1024,4096]{1,0:T(8,128)(2,1)} copy(bf16[1024,4096]{0,1:T(8,128)(2,1)} %bitcast.333) | data formatting | bytes 16777216 | tf_op jit(solution)/shard_map/dot_general | solution.py:113
  492.3 6.1 fusion.125
  502.2 5.8 fusion.13
  511.2 15.4 %reduce-scatter.6.cloned.1.call-done = bf16[64,1024]{1,0:T(8,128)(2,1)} async-done(((bf16[64,4096]{1,0:T(8,128)(2,1)}), bf16[64,1024]{1,0:T(8,128)(2,1)}) %reduce-scatter.6.cloned.1.call-update) | async-done | bytes 131088 | tf_op jit(solution)/shard_map/reduce_scatter | solution.py:160
  531.9 13.5 %all_gather.64 = bf16[64,4096]{1,0:T(8,128)(2,1)S(1)} all-gather(bf16[64,1024]{1,0:T(8,128)(2,1)S(1)} %fusion.65), channel_id=1, replica_groups=mesh['section'=2,'blk'=16,'mp'=4] {'mp'}, dimensions={1}, use_global_device_ids=true | all-gather | bytes 655360 | tf_op jit(solution)/shard_map/all_gather | solution.py:105
  546.5 6.1 fusion.128
  552.6 23.8 %all-gather.1 = bf16[1024,1,1,128]{3,0,2,1:T(8,128)(2,1)S(1)} all-gather(bf16[64,1,1,128]{3,0,2,1:T(8,128)(2,1)S(1)} %slice.284), channel_id=3, replica_groups=mesh['section'=2,'blk'=16,'mp'=4] {'blk'}, dimensions={0}, use_global_device_ids=true | all-gather | bytes 278528 | tf_op jit(solution)/shard_map/all_gather | solution.py:128
  576.7 23.3 %all_gather.66 = bf16[1024,1,128]{2,0,1:T(8,128)(2,1)S(1)} all-gather(bf16[64,1,128]{2,0,1:T(8,128)(2,1)S(1)} %pad_maximum_fusion.1), channel_id=1, replica_groups=mesh['section'=2,'blk'=16,'mp'=4] {'blk'}, dimensions={0}, use_global_device_ids=true | all-gather | bytes 278528 | tf_op jit(solution)/shard_map/all_gather | solution.py:127
  616.2 14.5 %reduce-scatter.8.cloned.1.call-done = bf16[64,1024]{1,0:T(8,128)(2,1)} async-done(((bf16[64,4096]{1,0:T(8,128)(2,1)}), bf16[64,1024]{1,0:T(8,128)(2,1)}) %reduce-scatter.8.cloned.1.call-update) | async-done | bytes 131088 | tf_op jit(solution)/shard_map/reduce_scatter | solution.py:160
  633.9 13.5 %all_gather.67 = bf16[64,4096]{1,0:T(8,128)(2,1)S(1)} all-gather(bf16[64,1024]{1,0:T(8,128)(2,1)S(1)} %broadcast_select_fusion.2), channel_id=1, replica_groups=mesh['section'=2,'blk'=16,'mp'=4] {'mp'}, dimensions={1}, use_global_device_ids=true | all-gather | bytes 655360 | tf_op jit(solution)/shard_map/all_gather | solution.py:105
  648.5 6.1 fusion.131
  654.6 23.8 %all-gather.2 = bf16[1024,1,1,128]{3,0,2,1:T(8,128)(2,1)S(1)} all-gather(bf16[64,1,1,128]{3,0,2,1:T(8,128)(2,1)S(1)} %slice.283), channel_id=4, replica_groups=mesh['section'=2,'blk'=16,'mp'=4] {'blk'}, dimensions={0}, use_global_device_ids=true | all-gather | bytes 278528 | tf_op jit(solution)/shard_map/all_gather | solution.py:128
  678.7 23.4 %all_gather.69 = bf16[1024,1,128]{2,0,1:T(8,128)(2,1)S(1)} all-gather(bf16[64,1,128]{2,0,1:T(8,128)(2,1)S(1)} %pad_maximum_fusion.2), channel_id=1, replica_groups=mesh['section'=2,'blk'=16,'mp'=4] {'blk'}, dimensions={0}, use_global_device_ids=true | all-gather | bytes 278528 | tf_op jit(solution)/shard_map/all_gather | solution.py:127
  715.8 17.7 %reduce-scatter.10.cloned.1.call-done = bf16[64,1024]{1,0:T(8,128)(2,1)} async-done(((bf16[64,4096]{1,0:T(8,128)(2,1)}), bf16[64,1024]{1,0:T(8,128)(2,1)}) %reduce-scatter.10.cloned.1.call-update) | async-done | bytes 131088 | tf_op jit(solution)/shard_map/reduce_scatter | solution.py:160
  737.7 13.4 %all_gather.70 = bf16[64,4096]{1,0:T(8,128)(2,1)S(1)} all-gather(bf16[64,1024]{1,0:T(8,128)(2,1)S(1)} %broadcast_select_fusion.1), channel_id=1, replica_groups=mesh['section'=2,'blk'=16,'mp'=4] {'mp'}, dimensions={1}, use_global_device_ids=true | all-gather | bytes 655360 | tf_op jit(solution)/shard_map/all_gather | solution.py:105
  752.1 6.1 fusion.134
  758.2 23.8 %all-gather.3 = bf16[1024,1,1,128]{3,0,2,1:T(8,128)(2,1)S(1)} all-gather(bf16[64,1,1,128]{3,0,2,1:T(8,128)(2,1)S(1)} %slice.282), channel_id=5, replica_groups=mesh['section'=2,'blk'=16,'mp'=4] {'blk'}, dimensions={0}, use_global_device_ids=true | all-gather | bytes 278528 | tf_op jit(solution)/shard_map/all_gather | solution.py:128
  782.3 23.2 %all_gather.72 = bf16[1024,1,128]{2,0,1:T(8,128)(2,1)S(1)} all-gather(bf16[64,1,128]{2,0,1:T(8,128)(2,1)S(1)} %pad_maximum_fusion.3), channel_id=1, replica_groups=mesh['section'=2,'blk'=16,'mp'=4] {'blk'}, dimensions={0}, use_global_device_ids=true | all-gather | bytes 278528 | tf_op jit(solution)/shard_map/all_gather | solution.py:127
  809.1 2.9 fusion.314
  818.7 18.8 %reduce-scatter.12.cloned.1.call-done = bf16[64,1024]{1,0:T(8,128)(2,1)} async-done(((bf16[64,4096]{1,0:T(8,128)(2,1)}), bf16[64,1024]{1,0:T(8,128)(2,1)}) %reduce-scatter.12.cloned.1.call-update) | async-done | bytes 131088 | tf_op jit(solution)/shard_map/reduce_scatter | solution.py:160
  844.1 12.8 %all_gather.73 = bf16[64,4096]{1,0:T(8,128)(2,1)S(1)} all-gather(bf16[64,1024]{1,0:T(8,128)(2,1)S(1)} %broadcast_select_fusion), channel_id=1, replica_groups=mesh['section'=2,'blk'=16,'mp'=4] {'mp'}, dimensions={1}, use_global_device_ids=true | all-gather | bytes 655360 | tf_op jit(solution)/shard_map/all_gather | solution.py:105
  857.9 6.1 fusion.137
  864.0 23.8 %all-gather.4 = bf16[1024,1,1,128]{3,0,2,1:T(8,128)(2,1)S(1)} all-gather(bf16[64,1,1,128]{3,0,2,1:T(8,128)(2,1)S(1)} %slice.281), channel_id=6, replica_groups=mesh['section'=2,'blk'=16,'mp'=4] {'blk'}, dimensions={0}, use_global_device_ids=true | all-gather | bytes 278528 | tf_op jit(solution)/shard_map/all_gather | solution.py:128
  888.0 23.3 %all_gather.75 = bf16[1024,1,128]{2,0,1:T(8,128)(2,1)S(1)} all-gather(bf16[64,1,128]{2,0,1:T(8,128)(2,1)S(1)} %pad_maximum_fusion.4), channel_id=1, replica_groups=mesh['section'=2,'blk'=16,'mp'=4] {'blk'}, dimensions={0}, use_global_device_ids=true | all-gather | bytes 278528 | tf_op jit(solution)/shard_map/all_gather | solution.py:127
  922.1 18.1 %reduce-scatter.14.cloned.1.call-done = bf16[64,1024]{1,0:T(8,128)(2,1)} async-done(((bf16[64,4096]{1,0:T(8,128)(2,1)}), bf16[64,1024]{1,0:T(8,128)(2,1)}) %reduce-scatter.14.cloned.1.call-update) | async-done | bytes 131088 | tf_op jit(solution)/shard_map/reduce_scatter | solution.py:160
  (308 shorter events, 102.9 us)
Async XLA Ops:
  6.5 419.6 %all-gather.9.cloned.1.call-start = ((), (), s32[]{:S(2)}) async-start(), calls=%async_computation.5 | async-start | bytes 2228224 | tf_op jit(solution)/shard_map/all_gather | solution.py:74
  7.3 473.2 %all-gather.11.cloned.1.call-start = ((), (), s32[]{:S(2)}) async-start(), calls=%async_computation.6 | async-start | bytes 8912896 | tf_op jit(solution)/shard_map/all_gather | solution.py:73
  8.0 494.1 %all-gather.13.cloned.1.call-start = ((), (), s32[]{:S(2)}) async-start(), calls=%async_computation.7 | async-start | bytes 8912896 | tf_op jit(solution)/shard_map/all_gather | solution.py:75
  8.7 517.9 %reduce-scatter.6.cloned.1.call-start = ((), (), s32[]{:S(2)}) async-start(), calls=%async_computation.8 | async-start | bytes 655360 | tf_op jit(solution)/shard_map/reduce_scatter | solution.py:160
  21.4 385.4 %copy-start.25 = (s32[256]{0:T(256)S(1)}, s32[256]{0:T(256)}, u32[]{:S(2)}) copy-start(s32[256]{0:T(256)} %param.18) | copy-start | bytes 3076
  21.4 403.2 %slice-start.8 = ((s32[4096]{0:T(1024)}), s32[1024]{0:T(1024)S(1)}, s32[]{:S(2)}) async-start(s32[4096]{0:T(1024)} %param.19), calls=%async_computation.21 | async-start | bytes 8192 | tf_op jit(solution)/shard_map/slice | solution.py:149
  21.4 404.6 %copy-start.46 = (f32[64]{0:T(128)}, f32[64]{0:T(128)S(1)}, u32[]{:S(2)}) copy-start(f32[64]{0:T(128)S(1)} %get-tuple-element.74) | copy-start | bytes 772
  22.2 554.2 %copy-start.26 = (f32[64]{0:T(128)}, f32[64]{0:T(128)S(1)}, u32[]{:S(2)}) copy-start(f32[64]{0:T(128)S(1)} %multiply_exponential_fusion) | copy-start | bytes 772
  22.2 384.6 %copy-start.44 = (s32[64]{0:T(128)}, s32[64]{0:T(128)S(1)}, u32[]{:S(2)}) copy-start(s32[64]{0:T(128)S(1)} %iota_add_fusion.5) | copy-start | bytes 772
  22.3 384.5 %copy-start.29 = (s32[64]{0:T(128)}, s32[64]{0:T(128)S(1)}, u32[]{:S(2)}) copy-start(s32[64]{0:T(128)S(1)} %get-tuple-element.77) | copy-start | bytes 772
  22.3 403.8 %copy-start.40 = (f32[64]{0:T(128)}, f32[64]{0:T(128)S(1)}, u32[]{:S(2)}) copy-start(f32[64]{0:T(128)S(1)} %get-tuple-element.80) | copy-start | bytes 772
  22.3 403.8 %copy-start.42 = (f32[64]{0:T(128)}, f32[64]{0:T(128)S(1)}, u32[]{:S(2)}) copy-start(f32[64]{0:T(128)S(1)} %get-tuple-element.79) | copy-start | bytes 772
  22.3 384.5 %copy-start.32 = (s32[64]{0:T(128)}, s32[64]{0:T(128)S(1)}, u32[]{:S(2)}) copy-start(s32[64]{0:T(128)S(1)} %get-tuple-element.75) | copy-start | bytes 772
  22.3 384.5 %copy-start.34 = (s32[64]{0:T(128)}, s32[64]{0:T(128)S(1)}, u32[]{:S(2)}) copy-start(s32[64]{0:T(128)S(1)} %get-tuple-element.76) | copy-start | bytes 772
  22.3 403.7 %copy-start.36 = (f32[64]{0:T(128)}, f32[64]{0:T(128)S(1)}, u32[]{:S(2)}) copy-start(f32[64]{0:T(128)S(1)} %get-tuple-element.82) | copy-start | bytes 772
  22.4 403.7 %copy-start.38 = (f32[64]{0:T(128)}, f32[64]{0:T(128)S(1)}, u32[]{:S(2)}) copy-start(f32[64]{0:T(128)S(1)} %get-tuple-element.81) | copy-start | bytes 772
  508.0 122.6 %reduce-scatter.8.cloned.1.call-start = ((), (), s32[]{:S(2)}) async-start(), calls=%async_computation.9 | async-start | bytes 655360 | tf_op jit(solution)/shard_map/reduce_scatter | solution.py:160
  527.7 2.4 collective-permute-start
  546.5 56.9 %copy-start.21 = (f32[64,64]{1,0:T(8,128)S(1)}, f32[64,64]{1,0:T(8,128)}, u32[]{:S(2)}) copy-start(f32[64,64]{1,0:T(8,128)} %get-tuple-element.51) | copy-start | bytes 49156
  546.5 56.9 %copy-start.22 = (f32[64,64]{1,0:T(8,128)S(1)}, f32[64,64]{1,0:T(8,128)}, u32[]{:S(2)}) copy-start(f32[64,64]{1,0:T(8,128)} %get-tuple-element.52) | copy-start | bytes 49156
  546.5 57.1 %copy-start.14 = (pred[64,2048]{1,0:T(8,128)(4,1)S(1)}, pred[64,2048]{1,0:T(8,128)(4,1)}, u32[]{:S(2)}) copy-start(pred[64,2048]{1,0:T(8,128)(4,1)} %compare_and_fusion.1) | copy-start | bytes 393220
  611.8 121.7 %reduce-scatter.10.cloned.1.call-start = ((), (), s32[]{:S(2)}) async-start(), calls=%async_computation.10 | async-start | bytes 655360 | tf_op jit(solution)/shard_map/reduce_scatter | solution.py:160
  631.6 2.3 collective-permute-start.1
  648.5 57.1 %copy-start.19 = (f32[64,64]{1,0:T(8,128)S(1)}, f32[64,64]{1,0:T(8,128)}, u32[]{:S(2)}) copy-start(f32[64,64]{1,0:T(8,128)} %get-tuple-element.53) | copy-start | bytes 49156
  648.5 57.1 %copy-start.20 = (f32[64,64]{1,0:T(8,128)S(1)}, f32[64,64]{1,0:T(8,128)}, u32[]{:S(2)}) copy-start(f32[64,64]{1,0:T(8,128)} %get-tuple-element.54) | copy-start | bytes 49156
  648.5 57.2 %copy-start.13 = (pred[64,3072]{1,0:T(8,128)(4,1)S(1)}, pred[64,3072]{1,0:T(8,128)(4,1)}, u32[]{:S(2)}) copy-start(pred[64,3072]{1,0:T(8,128)(4,1)} %compare_and_fusion) | copy-start | bytes 589828
  714.5 122.9 %reduce-scatter.12.cloned.1.call-start = ((), (), s32[]{:S(2)}) async-start(), calls=%async_computation.11 | async-start | bytes 655360 | tf_op jit(solution)/shard_map/reduce_scatter | solution.py:160
  734.5 2.5 collective-permute-start.2
  752.1 56.9 %copy-start.17 = (f32[64,64]{1,0:T(8,128)S(1)}, f32[64,64]{1,0:T(8,128)}, u32[]{:S(2)}) copy-start(f32[64,64]{1,0:T(8,128)} %get-tuple-element.55) | copy-start | bytes 49156
  752.1 57.0 %copy-start.3 = (pred[64,4096]{1,0:T(8,128)(4,1)S(1)}, pred[64,4096]{1,0:T(8,128)(4,1)}, u32[]{:S(2)}) copy-start(pred[64,4096]{1,0:T(8,128)(4,1)} %get-tuple-element.40) | copy-start | bytes 786436
  818.6 121.5 %reduce-scatter.14.cloned.1.call-start = ((), (), s32[]{:S(2)}) async-start(), calls=%async_computation.12 | async-start | bytes 655360 | tf_op jit(solution)/shard_map/reduce_scatter | solution.py:160
  838.5 4.9 collective-permute-start.3
  (50 other events, 668.7 us)
Sparse Core Ops, SparseCore 0:
  9.5 47.7 all-gather.8
  59.5 74.0 all-gather.10
  135.7 81.8 all-gather.12
  508.1 18.4 reduce-scatter.5
  611.9 18.7 reduce-scatter.7
  714.6 18.8 reduce-scatter.9
  818.8 18.6 reduce-scatter.11
  921.4 18.7 reduce-scatter.13
where the time goes:
time: 957 us; the launch traced here: 949 us
  blocking collectives  685 us (72%)
  waiting for transfers between devices  87 us (9%)
  matrix products  81.5 us (9%)
  other arithmetic  37.5 us (4%)
  local copies, waits for them, and re-layouts  37.3 us (4%)
  between operations  15.1 us (2%)
    psum x1, blocking collectives, local(): merged_full = lax.psum(partial_merge, ('blk', 'mp')).astype(jnp.bfloat16)  383 us
    all_gather x5, blocking collectives, local(): lax.all_gather(new_values, 'blk', axis=0, tiled=True)  119 us
    all_gather x5, blocking collectives, local(): lax.all_gather(new_keys, 'blk', axis=0, tiled=True)  114 us
    reduce_scatter x5, waiting for transfers between devices, local(): lax.psum_scatter(term.astype(jnp.bfloat16), 'mp', scatter_dimension=1, ti...  84.4 us
    all_gather x5, blocking collectives, local(): features = lax.all_gather(incoming, 'mp', axis=1, tiled=True)  66.5 us
    dot_general x5, matrix products, local(): jnp.dot(normx, query_full, preferred_element_type=jnp.float32)  30.4 us
  transfers between devices with their start and end apart: 12, of which 6 were waited for; matrix products, arithmetic and copies ran while one was open for 7% of the time, Pallas kernels for 0%

commit v1 on v0

--- a/solution.py
+++ b/solution.py
@@ -5,6 +5,11 @@
 
 epsilon = 1e-06
 rope_base = 1000000.0
+
+
+def samples_tell(panel, mesh_ax, along_axis):
+    far_arr = lax.psum(panel, mesh_ax)
+    return lax.psum(far_arr, along_axis)
 
 
 def shifted(value, axis, by):
@@ -66,7 +71,7 @@
         jnp.dot(normed, merge_first, preferred_element_type=jnp.float32), approximate=False
     ).astype(jnp.bfloat16)
     partial_merge = jnp.dot(inner, merge_second, preferred_element_type=jnp.float32)
-    merged_full = lax.psum(partial_merge, ("blk", "mp")).astype(jnp.bfloat16)
+    merged_full = samples_tell(partial_merge, "blk", "mp").astype(jnp.bfloat16)
     merged_mine = lax.dynamic_slice_in_dim(merged_full, model_index * slice_width, slice_width, 1)
     visual_all = lax.all_gather(merged_mine, "section", axis=0, tiled=True)
     query_full, keyval_full, out_full = (

time: 957 us -> 770 us (0.80)
  blocking collectives: 685 us -> 346 us
  waiting for transfers between devices: 87 us -> 239 us
    psum x1, blocking collectives: 383 us -> 43 us  [samples_tell(): return lax.psum(far_arr, along_axis)]
    psum x0 -> x1, waiting for transfers between devices: none -> 86.1 us  [samples_tell(): far_arr = lax.psum(panel, mesh_ax)]
    all_gather x1, waiting for transfers between devices: 0.02 us -> 58.3 us  [local(): lax.all_gather(out_weight, 'blk', axis=2, tiled=True)]
  transfers between devices with their start and end apart: 12 -> 13, of which waited for: 6 -> 8; matrix products, arithmetic and copies ran while one was open for 7% -> 7% of each run, Pallas kernels for 0% -> 0%
where the time goes in v1:
time: 770 us; the launch traced here: 762 us
  blocking collectives  346 us (45%)
  waiting for transfers between devices  239 us (31%)
  matrix products  82 us (11%)
  other arithmetic  37.5 us (5%)
  local copies, waits for them, and re-layouts  37 us (5%)
  between operations  14.8 us (2%)
    all_gather x5, blocking collectives, local(): lax.all_gather(new_values, 'blk', axis=0, tiled=True)  117 us
    all_gather x5, blocking collectives, local(): lax.all_gather(new_keys, 'blk', axis=0, tiled=True)  117 us
    reduce_scatter x5, waiting for transfers between devices, local(): lax.psum_scatter(term.astype(jnp.bfloat16), 'mp', scatter_dimension=1, ti...  87.5 us
    psum x1, waiting for transfers between devices, samples_tell(): far_arr = lax.psum(panel, mesh_ax)  86.1 us
    all_gather x5, blocking collectives, local(): features = lax.all_gather(incoming, 'mp', axis=1, tiled=True)  66 us
    all_gather x1, waiting for transfers between devices, local(): lax.all_gather(out_weight, 'blk', axis=2, tiled=True)  58.3 us
    psum x1, blocking collectives, samples_tell(): return lax.psum(far_arr, along_axis)  43 us
    dot_general x5, matrix products, local(): jnp.dot(normx, query_full, preferred_element_type=jnp.float32)  30.7 us
  transfers between devices with their start and end apart: 13, of which 8 were waited for; matrix products, arithmetic and copies ran while one was open for 7% of the time, Pallas kernels for 0%

profile of v1, /device:TPU:0, one launch (start us, length us, event | category | flops | bytes accessed | tf_op | source)
XLA Modules:
  0.0 761.7 jit_solution(9915978230422649825)
XLA Ops:
  14.1 5.4 fusion.210
  26.0 86.1 %all-reduce.3.cloned.1.call-done = f32[128,4096]{1,0:T(8,128)} async-done(((f32[128,4096]{1,0:T(8,128)}), f32[128,4096]{1,0:T(8,128)}) %all-reduce.3.cloned.1.call-update) | async-done | bytes 2097168 | tf_op jit(solution)/shard_map/psum | solution.py:11
  112.1 43.0 %all-reduce.4 = bf16[128,4096]{1,0:T(8,128)(2,1)S(1)} all-reduce(f32[128,4096]{1,0:T(8,128)} %all-reduce.3.cloned.1.call-done), channel_id=1, replica_groups=mesh['section'=2,'blk'=16,'mp'=4] {'mp'}, use_global_device_ids=true, to_apply=%region_4.5 | all-reduce | flops 524288 | bytes 3145728 | tf_op jit(solution)/shard_map/psum | solution.py:12
  158.6 13.0 %all_gather.58 = bf16[64,4096]{1,0:T(8,128)(2,1)S(1)} all-gather(bf16[64,1024]{1,0:T(8,128)(2,1)S(1)} %fusion.63), channel_id=1, replica_groups=mesh['section'=2,'blk'=16,'mp'=4] {'mp'}, dimensions={1}, use_global_device_ids=true | all-gather | bytes 655360 | tf_op jit(solution)/shard_map/all_gather | solution.py:110
  177.7 24.0 %all_gather.61 = bf16[1024,1,128]{2,0,1:T(8,128)(2,1)S(1)} all-gather(bf16[64,1,128]{2,0,1:T(8,128)(2,1)S(1)} %pad_maximum_fusion), channel_id=1, replica_groups=mesh['section'=2,'blk'=16,'mp'=4] {'blk'}, dimensions={0}, use_global_device_ids=true | all-gather | bytes 278528 | tf_op jit(solution)/shard_map/all_gather | solution.py:132
  201.7 22.3 %all-gather = bf16[1024,1,1,128]{3,0,2,1:T(8,128)(2,1)S(1)} all-gather(bf16[64,1,1,128]{3,0,2,1:T(8,128)(2,1)S(1)} %slice.285), channel_id=2, replica_groups=mesh['section'=2,'blk'=16,'mp'=4] {'blk'}, dimensions={0}, use_global_device_ids=true | all-gather | bytes 278528 | tf_op jit(solution)/shard_map/all_gather | solution.py:133
  227.7 5.2 all-gather.11.cloned.1.call-done
  233.0 11.4 %copy.31 = bf16[1024,4096]{1,0:T(8,128)(2,1)} copy(bf16[1024,4096]{0,1:T(8,128)(2,1)} %bitcast.333) | data formatting | bytes 16777216 | tf_op jit(solution)/shard_map/dot_general | solution.py:118
  244.4 6.3 fusion.125
  254.6 58.3 %all-gather.13.cloned.1.call-done = bf16[1,1024,4096]{2,1,0:T(8,128)(2,1)} async-done(((bf16[1,1024,256]{2,1,0:T(8,128)(2,1)}), bf16[1,1024,4096]{2,1,0:T(8,128)(2,1)}) %all-gather.13.cloned.1.call-update) | async-done | bytes 8388624 | tf_op jit(solution)/shard_map/all_gather | solution.py:80
  312.9 5.8 fusion.13
  321.9 18.1 %reduce-scatter.6.cloned.1.call-done = bf16[64,1024]{1,0:T(8,128)(2,1)} async-done(((bf16[64,4096]{1,0:T(8,128)(2,1)}), bf16[64,1024]{1,0:T(8,128)(2,1)}) %reduce-scatter.6.cloned.1.call-update) | async-done | bytes 131088 | tf_op jit(solution)/shard_map/reduce_scatter | solution.py:165
  345.3 13.5 %all_gather.64 = bf16[64,4096]{1,0:T(8,128)(2,1)S(1)} all-gather(bf16[64,1024]{1,0:T(8,128)(2,1)S(1)} %fusion.65), channel_id=1, replica_groups=mesh['section'=2,'blk'=16,'mp'=4] {'mp'}, dimensions={1}, use_global_device_ids=true | all-gather | bytes 655360 | tf_op jit(solution)/shard_map/all_gather | solution.py:110
  359.8 6.1 fusion.128
  365.9 23.7 %all-gather.1 = bf16[1024,1,1,128]{3,0,2,1:T(8,128)(2,1)S(1)} all-gather(bf16[64,1,1,128]{3,0,2,1:T(8,128)(2,1)S(1)} %slice.284), channel_id=3, replica_groups=mesh['section'=2,'blk'=16,'mp'=4] {'blk'}, dimensions={0}, use_global_device_ids=true | all-gather | bytes 278528 | tf_op jit(solution)/shard_map/all_gather | solution.py:133
  389.9 23.3 %all_gather.66 = bf16[1024,1,128]{2,0,1:T(8,128)(2,1)S(1)} all-gather(bf16[64,1,128]{2,0,1:T(8,128)(2,1)S(1)} %pad_maximum_fusion.1), channel_id=1, replica_groups=mesh['section'=2,'blk'=16,'mp'=4] {'blk'}, dimensions={0}, use_global_device_ids=true | all-gather | bytes 278528 | tf_op jit(solution)/shard_map/all_gather | solution.py:132
  428.8 15.1 %reduce-scatter.8.cloned.1.call-done = bf16[64,1024]{1,0:T(8,128)(2,1)} async-done(((bf16[64,4096]{1,0:T(8,128)(2,1)}), bf16[64,1024]{1,0:T(8,128)(2,1)}) %reduce-scatter.8.cloned.1.call-update) | async-done | bytes 131088 | tf_op jit(solution)/shard_map/reduce_scatter | solution.py:165
  447.4 13.4 %all_gather.67 = bf16[64,4096]{1,0:T(8,128)(2,1)S(1)} all-gather(bf16[64,1024]{1,0:T(8,128)(2,1)S(1)} %broadcast_select_fusion.2), channel_id=1, replica_groups=mesh['section'=2,'blk'=16,'mp'=4] {'mp'}, dimensions={1}, use_global_device_ids=true | all-gather | bytes 655360 | tf_op jit(solution)/shard_map/all_gather | solution.py:110
  461.9 6.1 fusion.131
  468.0 23.7 %all-gather.2 = bf16[1024,1,1,128]{3,0,2,1:T(8,128)(2,1)S(1)} all-gather(bf16[64,1,1,128]{3,0,2,1:T(8,128)(2,1)S(1)} %slice.283), channel_id=4, replica_groups=mesh['section'=2,'blk'=16,'mp'=4] {'blk'}, dimensions={0}, use_global_device_ids=true | all-gather | bytes 278528 | tf_op jit(solution)/shard_map/all_gather | solution.py:133
  492.0 23.5 %all_gather.69 = bf16[1024,1,128]{2,0,1:T(8,128)(2,1)S(1)} all-gather(bf16[64,1,128]{2,0,1:T(8,128)(2,1)S(1)} %pad_maximum_fusion.2), channel_id=1, replica_groups=mesh['section'=2,'blk'=16,'mp'=4] {'blk'}, dimensions={0}, use_global_device_ids=true | all-gather | bytes 278528 | tf_op jit(solution)/shard_map/all_gather | solution.py:132
  529.1 17.6 %reduce-scatter.10.cloned.1.call-done = bf16[64,1024]{1,0:T(8,128)(2,1)} async-done(((bf16[64,4096]{1,0:T(8,128)(2,1)}), bf16[64,1024]{1,0:T(8,128)(2,1)}) %reduce-scatter.10.cloned.1.call-update) | async-done | bytes 131088 | tf_op jit(solution)/shard_map/reduce_scatter | solution.py:165
  550.9 13.3 %all_gather.70 = bf16[64,4096]{1,0:T(8,128)(2,1)S(1)} all-gather(bf16[64,1024]{1,0:T(8,128)(2,1)S(1)} %broadcast_select_fusion.1), channel_id=1, replica_groups=mesh['section'=2,'blk'=16,'mp'=4] {'mp'}, dimensions={1}, use_global_device_ids=true | all-gather | bytes 655360 | tf_op jit(solution)/shard_map/all_gather | solution.py:110
  565.4 6.1 fusion.134
  571.5 23.8 %all-gather.3 = bf16[1024,1,1,128]{3,0,2,1:T(8,128)(2,1)S(1)} all-gather(bf16[64,1,1,128]{3,0,2,1:T(8,128)(2,1)S(1)} %slice.282), channel_id=5, replica_groups=mesh['section'=2,'blk'=16,'mp'=4] {'blk'}, dimensions={0}, use_global_device_ids=true | all-gather | bytes 278528 | tf_op jit(solution)/shard_map/all_gather | solution.py:133
  595.5 23.2 %all_gather.72 = bf16[1024,1,128]{2,0,1:T(8,128)(2,1)S(1)} all-gather(bf16[64,1,128]{2,0,1:T(8,128)(2,1)S(1)} %pad_maximum_fusion.3), channel_id=1, replica_groups=mesh['section'=2,'blk'=16,'mp'=4] {'blk'}, dimensions={0}, use_global_device_ids=true | all-gather | bytes 278528 | tf_op jit(solution)/shard_map/all_gather | solution.py:132
  631.9 18.8 %reduce-scatter.12.cloned.1.call-done = bf16[64,1024]{1,0:T(8,128)(2,1)} async-done(((bf16[64,4096]{1,0:T(8,128)(2,1)}), bf16[64,1024]{1,0:T(8,128)(2,1)}) %reduce-scatter.12.cloned.1.call-update) | async-done | bytes 131088 | tf_op jit(solution)/shard_map/reduce_scatter | solution.py:165
  657.3 12.8 %all_gather.73 = bf16[64,4096]{1,0:T(8,128)(2,1)S(1)} all-gather(bf16[64,1024]{1,0:T(8,128)(2,1)S(1)} %broadcast_select_fusion), channel_id=1, replica_groups=mesh['section'=2,'blk'=16,'mp'=4] {'mp'}, dimensions={1}, use_global_device_ids=true | all-gather | bytes 655360 | tf_op jit(solution)/shard_map/all_gather | solution.py:110
  671.2 6.1 fusion.137
  677.2 23.7 %all-gather.4 = bf16[1024,1,1,128]{3,0,2,1:T(8,128)(2,1)S(1)} all-gather(bf16[64,1,1,128]{3,0,2,1:T(8,128)(2,1)S(1)} %slice.281), channel_id=6, replica_groups=mesh['section'=2,'blk'=16,'mp'=4] {'blk'}, dimensions={0}, use_global_device_ids=true | all-gather | bytes 278528 | tf_op jit(solution)/shard_map/all_gather | solution.py:133
  701.3 23.3 %all_gather.75 = bf16[1024,1,128]{2,0,1:T(8,128)(2,1)S(1)} all-gather(bf16[64,1,128]{2,0,1:T(8,128)(2,1)S(1)} %pad_maximum_fusion.4), channel_id=1, replica_groups=mesh['section'=2,'blk'=16,'mp'=4] {'blk'}, dimensions={0}, use_global_device_ids=true | all-gather | bytes 278528 | tf_op jit(solution)/shard_map/all_gather | solution.py:132
  735.3 18.0 %reduce-scatter.14.cloned.1.call-done = bf16[64,1024]{1,0:T(8,128)(2,1)} async-done(((bf16[64,4096]{1,0:T(8,128)(2,1)}), bf16[64,1024]{1,0:T(8,128)(2,1)}) %reduce-scatter.14.cloned.1.call-update) | async-done | bytes 131088 | tf_op jit(solution)/shard_map/reduce_scatter | solution.py:165
  (313 shorter events, 112.9 us)
Async XLA Ops:
  6.5 105.6 %all-reduce.3.cloned.1.call-start = ((), (), s32[]{:S(2)}) async-start(), calls=%async_computation.5 | async-start | bytes 4194304 | tf_op jit(solution)/shard_map/psum | solution.py:11
  19.4 138.0 %copy-start.26 = (s32[256]{0:T(256)S(1)}, s32[256]{0:T(256)}, u32[]{:S(2)}) copy-start(s32[256]{0:T(256)} %param.18) | copy-start | bytes 3076
  19.4 152.4 %all-gather.9.cloned.1.call-start = ((), (), s32[]{:S(2)}) async-start(), calls=%async_computation.6 | async-start | bytes 2228224 | tf_op jit(solution)/shard_map/all_gather | solution.py:79
  20.2 212.8 %all-gather.11.cloned.1.call-start = ((), (), s32[]{:S(2)}) async-start(), calls=%async_computation.7 | async-start | bytes 8912896 | tf_op jit(solution)/shard_map/all_gather | solution.py:78
  20.9 292.0 %all-gather.13.cloned.1.call-start = ((), (), s32[]{:S(2)}) async-start(), calls=%async_computation.8 | async-start | bytes 8912896 | tf_op jit(solution)/shard_map/all_gather | solution.py:80
  21.5 318.4 %reduce-scatter.6.cloned.1.call-start = ((), (), s32[]{:S(2)}) async-start(), calls=%async_computation.9 | async-start | bytes 655360 | tf_op jit(solution)/shard_map/reduce_scatter | solution.py:165
  21.6 133.5 %copy-start.47 = (f32[64]{0:T(128)}, f32[64]{0:T(128)S(1)}, u32[]{:S(2)}) copy-start(f32[64]{0:T(128)S(1)} %get-tuple-element.74) | copy-start | bytes 772
  22.4 367.2 %copy-start.27 = (f32[64]{0:T(128)}, f32[64]{0:T(128)S(1)}, u32[]{:S(2)}) copy-start(f32[64]{0:T(128)S(1)} %multiply_exponential_fusion) | copy-start | bytes 772
  22.4 132.7 %copy-start.45 = (s32[64]{0:T(128)}, s32[64]{0:T(128)S(1)}, u32[]{:S(2)}) copy-start(s32[64]{0:T(128)S(1)} %iota_add_fusion.5) | copy-start | bytes 772
  22.5 154.1 %copy-start.30 = (s32[64]{0:T(128)}, s32[64]{0:T(128)S(1)}, u32[]{:S(2)}) copy-start(s32[64]{0:T(128)S(1)} %get-tuple-element.77) | copy-start | bytes 772
  22.5 132.6 %copy-start.41 = (f32[64]{0:T(128)}, f32[64]{0:T(128)S(1)}, u32[]{:S(2)}) copy-start(f32[64]{0:T(128)S(1)} %get-tuple-element.80) | copy-start | bytes 772
  22.5 132.6 %copy-start.43 = (f32[64]{0:T(128)}, f32[64]{0:T(128)S(1)}, u32[]{:S(2)}) copy-start(f32[64]{0:T(128)S(1)} %get-tuple-element.79) | copy-start | bytes 772
  22.5 132.6 %copy-start.33 = (s32[64]{0:T(128)}, s32[64]{0:T(128)S(1)}, u32[]{:S(2)}) copy-start(s32[64]{0:T(128)S(1)} %get-tuple-element.75) | copy-start | bytes 772
  22.5 132.6 %copy-start.35 = (s32[64]{0:T(128)}, s32[64]{0:T(128)S(1)}, u32[]{:S(2)}) copy-start(s32[64]{0:T(128)S(1)} %get-tuple-element.76) | copy-start | bytes 772
  22.6 132.6 %copy-start.37 = (f32[64]{0:T(128)}, f32[64]{0:T(128)S(1)}, u32[]{:S(2)}) copy-start(f32[64]{0:T(128)S(1)} %get-tuple-element.82) | copy-start | bytes 772
  22.6 132.6 %copy-start.39 = (f32[64]{0:T(128)}, f32[64]{0:T(128)S(1)}, u32[]{:S(2)}) copy-start(f32[64]{0:T(128)S(1)} %get-tuple-element.81) | copy-start | bytes 772
  318.7 125.1 %reduce-scatter.8.cloned.1.call-start = ((), (), s32[]{:S(2)}) async-start(), calls=%async_computation.10 | async-start | bytes 655360 | tf_op jit(solution)/shard_map/reduce_scatter | solution.py:165
  341.0 2.4 collective-permute-start
  359.8 56.9 %copy-start.21 = (f32[64,64]{1,0:T(8,128)S(1)}, f32[64,64]{1,0:T(8,128)}, u32[]{:S(2)}) copy-start(f32[64,64]{1,0:T(8,128)} %get-tuple-element.51) | copy-start | bytes 49156
  359.8 57.0 %copy-start.14 = (pred[64,2048]{1,0:T(8,128)(4,1)S(1)}, pred[64,2048]{1,0:T(8,128)(4,1)}, u32[]{:S(2)}) copy-start(pred[64,2048]{1,0:T(8,128)(4,1)} %compare_and_fusion.1) | copy-start | bytes 393220
  425.0 121.7 %reduce-scatter.10.cloned.1.call-start = ((), (), s32[]{:S(2)}) async-start(), calls=%async_computation.11 | async-start | bytes 655360 | tf_op jit(solution)/shard_map/reduce_scatter | solution.py:165
  444.8 2.5 collective-permute-start.1
  461.8 57.1 %copy-start.19 = (f32[64,64]{1,0:T(8,128)S(1)}, f32[64,64]{1,0:T(8,128)}, u32[]{:S(2)}) copy-start(f32[64,64]{1,0:T(8,128)} %get-tuple-element.53) | copy-start | bytes 49156
  461.8 57.1 %copy-start.20 = (f32[64,64]{1,0:T(8,128)S(1)}, f32[64,64]{1,0:T(8,128)}, u32[]{:S(2)}) copy-start(f32[64,64]{1,0:T(8,128)} %get-tuple-element.54) | copy-start | bytes 49156
  461.9 57.2 %copy-start.13 = (pred[64,3072]{1,0:T(8,128)(4,1)S(1)}, pred[64,3072]{1,0:T(8,128)(4,1)}, u32[]{:S(2)}) copy-start(pred[64,3072]{1,0:T(8,128)(4,1)} %compare_and_fusion) | copy-start | bytes 589828
  527.9 122.8 %reduce-scatter.12.cloned.1.call-start = ((), (), s32[]{:S(2)}) async-start(), calls=%async_computation.12 | async-start | bytes 655360 | tf_op jit(solution)/shard_map/reduce_scatter | solution.py:165
  547.8 2.5 collective-permute-start.2
  565.3 56.9 %copy-start.17 = (f32[64,64]{1,0:T(8,128)S(1)}, f32[64,64]{1,0:T(8,128)}, u32[]{:S(2)}) copy-start(f32[64,64]{1,0:T(8,128)} %get-tuple-element.55) | copy-start | bytes 49156
  565.3 56.9 %copy-start.18 = (f32[64,64]{1,0:T(8,128)S(1)}, f32[64,64]{1,0:T(8,128)}, u32[]{:S(2)}) copy-start(f32[64,64]{1,0:T(8,128)} %get-tuple-element.56) | copy-start | bytes 49156
  565.3 57.0 %copy-start.3 = (pred[64,4096]{1,0:T(8,128)(4,1)S(1)}, pred[64,4096]{1,0:T(8,128)(4,1)}, u32[]{:S(2)}) copy-start(pred[64,4096]{1,0:T(8,128)(4,1)} %get-tuple-element.40) | copy-start | bytes 786436
  631.9 121.5 %reduce-scatter.14.cloned.1.call-start = ((), (), s32[]{:S(2)}) async-start(), calls=%async_computation.13 | async-start | bytes 655360 | tf_op jit(solution)/shard_map/reduce_scatter | solution.py:165
  651.7 4.9 collective-permute-start.3
  (52 other events, 743.2 us)
Sparse Core Ops, SparseCore 0:
  19.6 92.4 all-reduce.2
  114.5 44.1 all-gather.8
  161.1 71.8 all-gather.10
  235.2 77.6 all-gather.12
  318.8 21.0 reduce-scatter.5
  425.1 18.6 reduce-scatter.7
  528.0 18.7 reduce-scatter.9
  632.0 18.6 reduce-scatter.11
  734.6 18.6 reduce-scatter.13
